TPU v7x, 32 devices: a whole 2x2x4 slice. The times are simulated.
32 devices in a mesh: groups: 2 (over x), dp: 16 (over z, y, core).
Axes of the slice: x: 2, y: 2, z: 4, core: 2. Of those that a mesh axis runs over, the one named last changes fastest.
Arguments:
- inputs: bfloat16 [64, 128, 4096], P(('groups', 'dp')), parts along dimension 0, may hold values from -6 to 6
- outputs: bfloat16 [64, 128, 4096], P(('groups', 'dp')), parts along dimension 0, may hold values from -6 to 6
- lengths: int32 [64], P(('groups', 'dp')), parts along dimension 0, may hold values from 64 to 128
- labels: int32 [64], P(('groups', 'dp')), parts along dimension 0, may hold values from 0 to 13
- norm_gain: float32 [4096], replicated, may hold values from 0.1 to 1.9
- classifier: bfloat16 [4096, 14], replicated, may hold values from -0.09375 to 0.09375
- proj_in: bfloat16 [4096, 64], replicated, may hold values from -0.09375 to 0.09375
- proj_out: bfloat16 [4096, 128], replicated, may hold values from -0.09375 to 0.09375
- query_index: int32 [256], P('groups'), parts along dimension 0, may hold values from 0 to 31, as said below
- prior_fisher: float32 [16384, 8192], P('groups', 'dp'), parts along dimension 0, may hold values from -4 to 18, as said below
Outputs:
- influence: float32 [8192, 256], P('dp', 'groups'), parts along dimension 1
- scores: float32 [64, 128], P(('groups', 'dp')), parts along dimension 0
There are 2 independent parts, one for each index of `groups`. A program takes and returns all parts, laid end to end along the dimension named above; an argument that names none is the same for every part. Nothing has to cross between parts.
Inputs may be any that keep to these rules, and one draw needn't show every extreme that they name: `query_index`: indices may repeat. `prior_fisher`: symmetric and positive definite.
All inputs are finite; a program needn't handle non-finite values.
Results may differ from a plain program's by a relative error of at most 0.0044.
Values may be sent and summed in bfloat16 or wider, within the bound.
A program may use at most 128 MiB of HBM per device.

v0:
```python
import jax
import jax.numpy as jnp
from jax import lax
from jax.sharding import PartitionSpec as P

D = 4096
CLASSES = 14
ITERS = 4
norm_eps = 1e-05
damp_share = 0.5
highest = lax.Precision.HIGHEST


def project_rows(inputs, outputs, lengths, labels, norm_gain, classifier, proj_in, proj_out):
    ex_count = inputs.shape[0]
    tok_count = inputs.shape[1]
    hidden = outputs.astype(jnp.float32)
    root_mean = jnp.sqrt(jnp.mean(hidden * hidden, axis=-1, keepdims=True) + norm_eps)
    positions = jnp.arange(tok_count, dtype=jnp.int32)
    live_mask = (positions[None, :] < lengths[:, None]).astype(jnp.float32)[:, :, None]
    length_float = lengths.astype(jnp.float32)[:, None, None]
    normed = norm_gain * hidden / root_mean
    pooled = jnp.sum(live_mask * normed, axis=1) / length_float[:, 0]
    class_weight = classifier.astype(jnp.float32)
    logits = jnp.dot(pooled, class_weight, precision=highest)
    exponent = jnp.exp(logits)
    probs = exponent / jnp.sum(exponent, axis=-1, keepdims=True)
    target = (jnp.arange(CLASSES, dtype=jnp.int32)[None, :] == labels[:, None]).astype(jnp.float32)
    pooled_grad = lax.dot_general(
        probs - target, class_weight, (((1,), (1,)), ((), ())), precision=highest
    )
    scaled = norm_gain * (live_mask / length_float) * pooled_grad[:, None, :]
    out_grad = scaled / root_mean - hidden * jnp.sum(hidden * scaled, axis=-1, keepdims=True) / (
        D * root_mean**3
    )
    grad_low = out_grad.astype(jnp.bfloat16)
    input_proj = jnp.dot(
        inputs.reshape(ex_count * tok_count, D).astype(jnp.float32),
        proj_in.astype(jnp.float32),
        precision=highest,
    )
    grad_proj = jnp.dot(
        grad_low.reshape(ex_count * tok_count, D).astype(jnp.float32),
        proj_out.astype(jnp.float32),
        precision=highest,
    )
    input_proj = input_proj.reshape(ex_count, tok_count, -1)
    grad_proj = grad_proj.reshape(ex_count, tok_count, -1)
    outer = jnp.einsum("eta,etb->eab", input_proj, grad_proj, precision=highest)
    return outer.reshape(ex_count, -1).astype(jnp.bfloat16)


def conjugate(queries, apply_fisher, reduce_inner):
    solved = jnp.zeros_like(queries)
    residual = queries
    direction = queries
    norm_now = reduce_inner(residual, residual)
    for step_index in range(ITERS):
        image = apply_fisher(direction)
        alpha = norm_now / reduce_inner(direction, image)
        solved = solved + alpha * direction
        residual = residual - alpha * image
        norm_next = reduce_inner(residual, residual)
        direction = residual + norm_next / norm_now * direction
        norm_now = norm_next
    return solved


def pieces_inner(first_vec, second_vec):
    return lax.psum(jnp.sum(first_vec * second_vec, axis=0), "dp")


def contract_rows(left_rows, right_rows):
    return jnp.dot(
        left_rows.astype(jnp.float32).T, right_rows.astype(jnp.float32), precision=highest
    )


def body(
    inputs,
    outputs,
    lengths,
    labels,
    norm_gain,
    classifier,
    proj_in,
    proj_out,
    query_index,
    prior_fisher,
):
    own_rows = project_rows(
        inputs, outputs, lengths, labels, norm_gain, classifier, proj_in, proj_out
    )
    devices = lax.axis_size("dp")
    device_index = lax.axis_index("dp")
    own_count = own_rows.shape[0]
    total_rows = own_count * devices
    width = own_rows.shape[1]
    piece = width // devices
    own_float = own_rows.astype(jnp.float32)
    square_sum = lax.psum(jnp.sum(own_float * own_float), "dp")
    damping = damp_share * square_sum / (total_rows * total_rows)
    every = lax.all_gather(own_rows, "dp", axis=0, tiled=True)
    mine = lax.dynamic_slice_in_dim(every, device_index * piece, piece, 1)
    strip = contract_rows(every, mine) / total_rows + damping * prior_fisher

    def apply_piece(vectors):
        return lax.psum_scatter(
            jnp.dot(strip, vectors, precision=highest), "dp", scatter_dimension=0, tiled=True
        )

    queries = jnp.take(mine, query_index, axis=0).astype(jnp.float32).T
    solved = conjugate(queries, apply_piece, pieces_inner)
    block = mine.astype(jnp.float32)
    scores = lax.psum_scatter(
        jnp.dot(block, solved, precision=highest) / total_rows,
        "dp",
        scatter_dimension=0,
        tiled=True,
    )
    return (solved, scores)


def solution(mesh):
    return jax.shard_map(
        body,
        mesh=mesh,
        in_specs=(
            P(("groups", "dp"), None, None),
            P(("groups", "dp"), None, None),
            P(("groups", "dp")),
            P(("groups", "dp")),
            P(),
            P(),
            P(),
            P(),
            P("groups"),
            P("groups", "dp"),
        ),
        out_specs=(P("dp", "groups"), P(("groups", "dp"), None)),
        check_vma=False,
    )
```

profile of v0, /device:TPU:0, one launch (start us, length us, event | category | flops | bytes accessed | tf_op | source)
XLA Modules:
  0.0 715.0 jit_solution(6194514816210829395)
XLA Ops:
  10.2 2.1 fusion.6
  13.1 2.5 fusion.8
  16.3 2.1 fusion.3
  20.8 24.6 %all-gather = bf16[16,2,8192]{2,1,0:T(2,128)(2,1)S(1)} all-gather(bf16[1,2,8192]{2,1,0:T(2,128)(2,1)S(1)} %reshape.115), channel_id=1, replica_groups=mesh['groups'=2,'dp'=16] {'dp'}, dimensions={0}, use_global_device_ids=true | all-gather | bytes 557056 | tf_op jit(solution)/shard_map/all_gather | solution.py:103
  45.6 30.5 %psum.64 = f32[]{:T(128)} all-reduce(f32[]{:T(128)} %get-tuple-element.12), channel_id=1, replica_groups=mesh['groups'=2,'dp'=16] {'dp'}, use_global_device_ids=true, to_apply=%region_7.8 | all-reduce | flops 1 | bytes 8 | tf_op jit(solution)/shard_map/psum | solution.py:101
  77.7 8.1 %multiply_add_fusion = f32[8192,512]{1,0:T(8,128)S(1)} fusion(f32[8192,512]{1,0:T(8,128)} %param.19, bf16[32,8192]{1,0:T(8,128)(2,1)S(1)} %reshape.116, bf16[32,512]{1,0:T(8,128)(2,1)S(1)} %constant_dynamic-slice_fusion.1, f32[]{:T(128)S(6)} %div.104), kind=kOutput, calls=%fused_computation.2 | convolution fusion | flops 281018368 | bytes 34111492 | tf_op jit(solution)/shard_map/dot_general | solution.py:74
  85.9 5.7 copy-done.1
  91.6 9.1 %fusion.22 = f32[8192,128]{1,0:T(8,128)} fusion(f32[8192,512]{1,0:T(8,128)S(1)} %multiply_add_fusion, bf16[128,512]{0,1:T(8,128)(2,1)S(1)} %copy.13, pred[128]{0:T(512)(128)(4,1)S(1)} %compare_and_fusion), kind=kOutput, calls=%fused_computation.49 | convolution fusion | flops 6442516480 | bytes 21102720 | tf_op jit(solution)/shard_map/dot_general | solution.py:109
  100.7 69.7 %reduce-scatter.5.cloned.1.call-done = f32[512,128]{1,0:T(8,128)} async-done(((f32[8192,128]{1,0:T(8,128)}), f32[512,128]{1,0:T(8,128)}) %reduce-scatter.5.cloned.1.call-update) | async-done | bytes 262160 | tf_op jit(solution)/shard_map/reduce_scatter | solution.py:108
  171.5 30.4 %all-reduce.1 = (f32[128]{0:T(128)S(1)}, f32[128]{0:T(128)S(1)}) all-reduce(f32[128]{0:T(128)S(1)} %get-tuple-element.3, f32[128]{0:T(128)S(1)} %get-tuple-element.2), channel_id=1, replica_groups=mesh['groups'=2,'dp'=16] {'dp'}, use_global_device_ids=true, to_apply=%region_5.0 | all-reduce | flops 256 | bytes 2048 | tf_op jit(solution)/shard_map/psum | solution.py:70
  202.9 29.5 %psum.66 = f32[128]{0:T(128)S(1)} all-reduce(f32[128]{0:T(128)S(1)} %multiply_reduce_fusion.5), channel_id=1, replica_groups=mesh['groups'=2,'dp'=16] {'dp'}, use_global_device_ids=true, to_apply=%region_12.13 | all-reduce | flops 128 | bytes 1024 | tf_op jit(solution)/shard_map/psum | solution.py:70
  232.4 17.4 %fusion.31 = f32[8192,128]{1,0:T(8,128)} fusion(f32[8192,512]{1,0:T(8,128)} %copy-done.1, f32[512,128]{1,0:T(8,128)} %reduce-scatter.5.cloned.1.call-done, f32[128]{0:T(128)S(1)} %div.106, f32[128]{0:T(128)S(1)} %div.105, bf16[128,512]{0,1:T(8,128)(2,1)S(1)} %copy.13, pred[128]{0:T(512)(128)(4,1)S(1)} %compare_and_fusion), kind=kOutput, calls=%fused_computation.69 | convolution fusion | flops 6442844160 | bytes 21365888 | tf_op jit(solution)/shard_map/dot_general | solution.py:109
  249.9 69.6 %reduce-scatter.7.cloned.1.call-done = f32[512,128]{1,0:T(8,128)} async-done(((f32[8192,128]{1,0:T(8,128)}), f32[512,128]{1,0:T(8,128)}) %reduce-scatter.7.cloned.1.call-update) | async-done | bytes 262160 | tf_op jit(solution)/shard_map/reduce_scatter | solution.py:108
  320.6 30.1 %psum.67 = f32[128]{0:T(128)S(1)} all-reduce(f32[128]{0:T(128)S(1)} %multiply_reduce_fusion.4), channel_id=1, replica_groups=mesh['groups'=2,'dp'=16] {'dp'}, use_global_device_ids=true, to_apply=%region_15.16 | all-reduce | flops 128 | bytes 1024 | tf_op jit(solution)/shard_map/psum | solution.py:70
  350.7 1.0 multiply_reduce_fusion.3
  351.8 29.5 %psum.68 = f32[128]{0:T(128)S(1)} all-reduce(f32[128]{0:T(128)S(1)} %get-tuple-element.6), channel_id=1, replica_groups=mesh['groups'=2,'dp'=16] {'dp'}, use_global_device_ids=true, to_apply=%region_17.18 | all-reduce | flops 128 | bytes 1024 | tf_op jit(solution)/shard_map/psum | solution.py:70
  381.4 17.4 %fusion.34 = f32[8192,128]{1,0:T(8,128)} fusion(f32[8192,512]{1,0:T(8,128)} %copy-done.1, f32[512,128]{1,0:T(8,128)S(1)} %multiply_add_fusion.2), kind=kOutput, calls=%fused_computation.71 | convolution fusion | flops 6442450944 | bytes 21233664 | tf_op jit(solution)/shard_map/dot_general | solution.py:109
  398.8 69.7 %reduce-scatter.9.cloned.1.call-done = f32[512,128]{1,0:T(8,128)} async-done(((f32[8192,128]{1,0:T(8,128)}), f32[512,128]{1,0:T(8,128)}) %reduce-scatter.9.cloned.1.call-update) | async-done | bytes 262160 | tf_op jit(solution)/shard_map/reduce_scatter | solution.py:108
  469.6 30.1 %psum.69 = f32[128]{0:T(128)S(1)} all-reduce(f32[128]{0:T(128)S(1)} %multiply_reduce_fusion.2), channel_id=1, replica_groups=mesh['groups'=2,'dp'=16] {'dp'}, use_global_device_ids=true, to_apply=%region_20.21 | all-reduce | flops 128 | bytes 1024 | tf_op jit(solution)/shard_map/psum | solution.py:70
  500.8 29.7 %psum.70 = f32[128]{0:T(128)S(1)} all-reduce(f32[128]{0:T(128)S(1)} %multiply_reduce_fusion.1), channel_id=1, replica_groups=mesh['groups'=2,'dp'=16] {'dp'}, use_global_device_ids=true, to_apply=%region_22.23 | all-reduce | flops 128 | bytes 1024 | tf_op jit(solution)/shard_map/psum | solution.py:70
  531.5 17.4 %fusion.35 = f32[8192,128]{1,0:T(8,128)} fusion(f32[8192,512]{1,0:T(8,128)} %copy-done.1, f32[512,128]{1,0:T(8,128)S(1)} %multiply_add_fusion.1), kind=kOutput, calls=%fused_computation.72 | convolution fusion | flops 6442450944 | bytes 21233664 | tf_op jit(solution)/shard_map/dot_general | solution.py:109
  550.8 68.0 %reduce-scatter.11.cloned.1.call-done = f32[512,128]{1,0:T(8,128)} async-done(((f32[8192,128]{1,0:T(8,128)}), f32[512,128]{1,0:T(8,128)}) %reduce-scatter.11.cloned.1.call-update) | async-done | bytes 262160 | tf_op jit(solution)/shard_map/reduce_scatter | solution.py:108
  619.9 30.1 %psum.71 = f32[128]{0:T(128)S(1)} all-reduce(f32[128]{0:T(128)S(1)} %multiply_reduce_fusion), channel_id=1, replica_groups=mesh['groups'=2,'dp'=16] {'dp'}, use_global_device_ids=true, to_apply=%region_25.26 | all-reduce | flops 128 | bytes 1024 | tf_op jit(solution)/shard_map/psum | solution.py:70
  650.3 57.6 %all-reduce = f32[32,128]{1,0:T(8,128)S(1)} all-reduce(f32[32,128]{1,0:T(8,128)S(1)} %convolution_multiply_fusion), channel_id=6, replica_groups=mesh['groups'=2,'dp'=16] {'dp'}, use_global_device_ids=true, to_apply=%region_26.27.clone | all-reduce | flops 4096 | bytes 32768
  (64 shorter events, 17.6 us)
Async XLA Ops:
  7.2 12.0 %copy-start = (bf16[2,128,4096]{2,1,0:T(8,128)(2,1)S(1)}, bf16[2,128,4096]{2,1,0:T(8,128)(2,1)}, u32[]{:S(2)}) copy-start(bf16[2,128,4096]{2,1,0:T(8,128)(2,1)} %param.10) | copy-start | bytes 6291460
  7.2 9.1 %copy-start.7 = (f32[4096]{0:T(1024)S(1)}, f32[4096]{0:T(1024)}, u32[]{:S(2)}) copy-start(f32[4096]{0:T(1024)} %param.14) | copy-start | bytes 49156
  7.2 8.4 %copy-start.8 = (bf16[4096,14]{0,1:T(8,128)(2,1)S(1)}, bf16[4096,14]{0,1:T(8,128)(2,1)}, u32[]{:S(2)}) copy-start(bf16[4096,14]{0,1:T(8,128)(2,1)} %param.15) | copy-start | bytes 344068
  7.2 8.8 %copy-start.9 = (s32[2]{0:T(128)S(1)}, s32[2]{0:T(128)}, u32[]{:S(2)}) copy-start(s32[2]{0:T(128)} %param.13) | copy-start | bytes 28
  7.2 163.2 %reduce-scatter.5.cloned.1.call-start = ((), (), s32[]{:S(2)}) async-start(), calls=%async_computation.4 | async-start | bytes 4456448 | tf_op jit(solution)/shard_map/reduce_scatter | solution.py:108
  7.3 9.1 %copy-start.3 = (bf16[2,128,4096]{2,1,0:T(8,128)(2,1)S(1)}, bf16[2,128,4096]{2,1,0:T(8,128)(2,1)}, u32[]{:S(2)}) copy-start(bf16[2,128,4096]{2,1,0:T(8,128)(2,1)} %param.11) | copy-start | bytes 6291460
  16.3 2.1 copy-start.4
  16.3 2.8 copy-start.6
  85.8 5.7 copy-start.1
  100.7 218.9 %reduce-scatter.7.cloned.1.call-start = ((), (), s32[]{:S(2)}) async-start(), calls=%async_computation.5 | async-start | bytes 4456448 | tf_op jit(solution)/shard_map/reduce_scatter | solution.py:108
  249.8 69.7 %copy-start.2 = (f32[512,128]{1,0:T(8,128)S(1)}, f32[512,128]{1,0:T(8,128)}, u32[]{:S(2)}) copy-start(f32[512,128]{1,0:T(8,128)} %reduce-scatter.5.cloned.1.call-done) | copy-start | bytes 786436
  249.8 218.7 %reduce-scatter.9.cloned.1.call-start = ((), (), s32[]{:S(2)}) async-start(), calls=%async_computation.6 | async-start | bytes 4456448 | tf_op jit(solution)/shard_map/reduce_scatter | solution.py:108
  398.8 220.0 %reduce-scatter.11.cloned.1.call-start = ((), (), s32[]{:S(2)}) async-start(), calls=%async_computation.7 | async-start | bytes 4456448 | tf_op jit(solution)/shard_map/reduce_scatter | solution.py:108
  548.9 0.7 copy-start.10
  650.0 58.4 %copy-start.5 = (f32[512,128]{1,0:T(8,128)}, f32[512,128]{1,0:T(8,128)S(1)}, u32[]{:S(2)}) copy-start(f32[512,128]{1,0:T(8,128)S(1)} %fusion.20) | copy-start | bytes 786436
Sparse Core Ops, SparseCore 0:
  100.8 69.6 reduce-scatter.4
  250.0 69.5 reduce-scatter.6
  398.9 69.6 reduce-scatter.8
  549.1 69.7 reduce-scatter.10
where the time goes:
time: 716 us; the launch traced here: 715 us
  blocking collectives  322 us (45%)
  waiting for transfers between devices  277 us (39%)
  matrix products  72.7 us (10%)
  other arithmetic  18.8 us (3%)
  between operations  15.3 us (2%)
  local copies, waits for them, and re-layouts  8.71 us (1%)
    reduce_scatter x4, waiting for transfers between devices, apply_piece(): lax.psum_scatter(jnp.dot(strip, vectors, precision=highest), 'dp', scatte...  277 us
    psum x7, blocking collectives, pieces_inner(): return lax.psum(jnp.sum(first_vec * second_vec, axis=0), 'dp')  209 us
    dot_general x4, matrix products, apply_piece(): jnp.dot(strip, vectors, precision=highest)  61.4 us
    unnamed x1, blocking collectives  57.6 us
    psum x1, blocking collectives, body(): square_sum = lax.psum(jnp.sum(own_float * own_float), 'dp')  30.5 us
    all_gather x1, blocking collectives, body(): every = lax.all_gather(own_rows, 'dp', axis=0, tiled=True)  24.6 us
  transfers between devices with their start and end apart: 4, of which 4 were waited for; matrix products, arithmetic and copies ran while one was open for 0% of the time, Pallas kernels for 0%

commit v1 on v0

--- a/solution.py
+++ b/solution.py
@@ -9,6 +9,19 @@
 norm_eps = 1e-05
 damp_share = 0.5
 highest = lax.Precision.HIGHEST
+
+
+def gather_around(x, axis, dim):
+    ways = lax.axis_size(axis)
+    up = [(d, (d + 1) % ways) for d in range(ways)]
+    down = [(d, (d - 1) % ways) for d in range(ways)]
+    earlier, later = ([x], [x])
+    for _ in range(ways // 2):
+        earlier.append(lax.ppermute(earlier[-1], axis, up))
+    for _ in range((ways - 1) // 2):
+        later.append(lax.ppermute(later[-1], axis, down))
+    line = jnp.concatenate([*earlier[::-1], *later[1:]], axis=dim)
+    return jnp.roll(line, (lax.axis_index(axis) - ways // 2) * x.shape[dim], axis=dim)
 
 
 def project_rows(inputs, outputs, lengths, labels, norm_gain, classifier, proj_in, proj_out):
@@ -100,7 +113,7 @@
     own_float = own_rows.astype(jnp.float32)
     square_sum = lax.psum(jnp.sum(own_float * own_float), "dp")
     damping = damp_share * square_sum / (total_rows * total_rows)
-    every = lax.all_gather(own_rows, "dp", axis=0, tiled=True)
+    every = gather_around(own_rows, "dp", 0)
     mine = lax.dynamic_slice_in_dim(every, device_index * piece, piece, 1)
     strip = contract_rows(every, mine) / total_rows + damping * prior_fisher
 

time: 716 us -> 744 us (1.039)
  starting transfers between devices: 0.16 us -> 32.4 us
  blocking collectives: 322 us -> 302 us
  waiting for transfers between devices: 277 us -> 289 us
    ppermute x0 -> x15, starting transfers between devices: none -> 32.2 us  [the longest x7 31.7 us: gather_around(): later.append(lax.ppermute(later[-1], axis, down))]
    all_gather x1 -> x0, blocking collectives: 24.6 us -> none  [body(): every = lax.all_gather(own_rows, 'dp', axis=0, tiled=True)]
    ppermute x0 -> x15, waiting for transfers between devices: none -> 11.1 us  [the longest x8 10.7 us: gather_around(): earlier.append(lax.ppermute(earlier[-1], axis, up))]
  transfers between devices with their start and end apart: 4 -> 19, of which waited for: 4 -> 17; matrix products, arithmetic and copies ran while one was open for 0% -> 0% of each run, Pallas kernels for 0% -> 0%
where the time goes in v1:
time: 744 us; the launch traced here: 743 us
  blocking collectives  302 us (41%)
  waiting for transfers between devices  289 us (39%)
  matrix products  72.8 us (10%)
  starting transfers between devices  32.4 us (4%)
  other arithmetic  17.5 us (2%)
  between operations  15.4 us (2%)
  local copies, waits for them, and re-layouts  13.9 us (2%)
    reduce_scatter x4, waiting for transfers between devices, apply_piece(): lax.psum_scatter(jnp.dot(strip, vectors, precision=highest), 'dp', scatte...  278 us
    psum x7, blocking collectives, pieces_inner(): return lax.psum(jnp.sum(first_vec * second_vec, axis=0), 'dp')  209 us
    dot_general x4, matrix products, apply_piece(): jnp.dot(strip, vectors, precision=highest)  61.4 us
    unnamed x1, blocking collectives  57.6 us
    psum x1, blocking collectives, body(): square_sum = lax.psum(jnp.sum(own_float * own_float), 'dp')  34.7 us
    ppermute x7, starting transfers between devices, gather_around(): later.append(lax.ppermute(later[-1], axis, down))  31.7 us
  transfers between devices with their start and end apart: 19, of which 17 were waited for; matrix products, arithmetic and copies ran while one was open for 0% of the time, Pallas kernels for 0%

profile of v1, /device:TPU:0, one launch (start us, length us, event | category | flops | bytes accessed | tf_op | source)
XLA Modules:
  0.0 742.7 jit_solution(4502224137481339887)
XLA Ops:
  20.0 5.1 collective-permute-start.8
  26.7 4.4 collective-permute-start.9
  50.8 4.4 collective-permute-start.13
  56.9 4.4 collective-permute-start.14
  62.9 34.7 %psum.64 = f32[]{:T(128)} all-reduce(f32[]{:T(128)} %get-tuple-element.12), channel_id=1, replica_groups=mesh['groups'=2,'dp'=16] {'dp'}, use_global_device_ids=true, to_apply=%region_7.8 | all-reduce | flops 1 | bytes 8 | tf_op jit(solution)/shard_map/psum | solution.py:114
  98.9 4.7 concatenate.6
  104.6 8.2 %multiply_add_fusion = f32[8192,512]{1,0:T(8,128)S(1)} fusion(f32[8192,512]{1,0:T(8,128)} %param.19, bf16[32,512]{1,0:T(8,128)(2,1)S(1)} %dynamic_slice.7, f32[]{:T(128)S(6)} %div.104, bf16[64,8192]{1,0:T(8,128)(2,1)S(1)} %concatenate.6, s32[]{:T(128)S(6)} %select_n.33), kind=kOutput, calls=%fused_computation.2 | convolution fusion | flops 281018368 | bytes 34111496 | tf_op jit(solution)/shard_map/dot_general | solution.py:87
  112.8 5.7 copy-done.1
  118.5 9.1 %fusion.23 = f32[8192,128]{1,0:T(8,128)} fusion(f32[8192,512]{1,0:T(8,128)S(1)} %multiply_add_fusion, bf16[128,512]{0,1:T(8,128)(2,1)S(1)} %copy.13, pred[128]{0:T(512)(128)(4,1)S(1)} %compare_and_fusion), kind=kOutput, calls=%fused_computation.50 | convolution fusion | flops 6442516480 | bytes 21102720 | tf_op jit(solution)/shard_map/dot_general | solution.py:122
  127.7 70.3 %reduce-scatter.5.cloned.1.call-done = f32[512,128]{1,0:T(8,128)} async-done(((f32[8192,128]{1,0:T(8,128)}), f32[512,128]{1,0:T(8,128)}) %reduce-scatter.5.cloned.1.call-update) | async-done | bytes 262160 | tf_op jit(solution)/shard_map/reduce_scatter | solution.py:121
  199.0 30.1 %all-reduce.1 = (f32[128]{0:T(128)S(1)}, f32[128]{0:T(128)S(1)}) all-reduce(f32[128]{0:T(128)S(1)} %get-tuple-element.3, f32[128]{0:T(128)S(1)} %get-tuple-element.2), channel_id=1, replica_groups=mesh['groups'=2,'dp'=16] {'dp'}, use_global_device_ids=true, to_apply=%region_5.0 | all-reduce | flops 256 | bytes 2048 | tf_op jit(solution)/shard_map/psum | solution.py:83
  230.1 29.7 %psum.66 = f32[128]{0:T(128)S(1)} all-reduce(f32[128]{0:T(128)S(1)} %multiply_reduce_fusion.5), channel_id=1, replica_groups=mesh['groups'=2,'dp'=16] {'dp'}, use_global_device_ids=true, to_apply=%region_12.13 | all-reduce | flops 128 | bytes 1024 | tf_op jit(solution)/shard_map/psum | solution.py:83
  259.8 17.4 %fusion.33 = f32[8192,128]{1,0:T(8,128)} fusion(f32[8192,512]{1,0:T(8,128)} %copy-done.1, f32[512,128]{1,0:T(8,128)} %reduce-scatter.5.cloned.1.call-done, f32[128]{0:T(128)S(1)} %div.106, f32[128]{0:T(128)S(1)} %div.105, bf16[128,512]{0,1:T(8,128)(2,1)S(1)} %copy.13, pred[128]{0:T(512)(128)(4,1)S(1)} %compare_and_fusion), kind=kOutput, calls=%fused_computation.71 | convolution fusion | flops 6442844160 | bytes 21365888 | tf_op jit(solution)/shard_map/dot_general | solution.py:122
  277.3 69.7 %reduce-scatter.7.cloned.1.call-done = f32[512,128]{1,0:T(8,128)} async-done(((f32[8192,128]{1,0:T(8,128)}), f32[512,128]{1,0:T(8,128)}) %reduce-scatter.7.cloned.1.call-update) | async-done | bytes 262160 | tf_op jit(solution)/shard_map/reduce_scatter | solution.py:121
  348.0 30.2 %psum.67 = f32[128]{0:T(128)S(1)} all-reduce(f32[128]{0:T(128)S(1)} %multiply_reduce_fusion.4), channel_id=1, replica_groups=mesh['groups'=2,'dp'=16] {'dp'}, use_global_device_ids=true, to_apply=%region_15.16 | all-reduce | flops 128 | bytes 1024 | tf_op jit(solution)/shard_map/psum | solution.py:83
  379.2 29.5 %psum.68 = f32[128]{0:T(128)S(1)} all-reduce(f32[128]{0:T(128)S(1)} %get-tuple-element.6), channel_id=1, replica_groups=mesh['groups'=2,'dp'=16] {'dp'}, use_global_device_ids=true, to_apply=%region_17.18 | all-reduce | flops 128 | bytes 1024 | tf_op jit(solution)/shard_map/psum | solution.py:83
  408.8 17.4 %fusion.36 = f32[8192,128]{1,0:T(8,128)} fusion(f32[8192,512]{1,0:T(8,128)} %copy-done.1, f32[512,128]{1,0:T(8,128)S(1)} %multiply_add_fusion.2), kind=kOutput, calls=%fused_computation.73 | convolution fusion | flops 6442450944 | bytes 21233664 | tf_op jit(solution)/shard_map/dot_general | solution.py:122
  426.3 70.0 %reduce-scatter.9.cloned.1.call-done = f32[512,128]{1,0:T(8,128)} async-done(((f32[8192,128]{1,0:T(8,128)}), f32[512,128]{1,0:T(8,128)}) %reduce-scatter.9.cloned.1.call-update) | async-done | bytes 262160 | tf_op jit(solution)/shard_map/reduce_scatter | solution.py:121
  497.4 30.1 %psum.69 = f32[128]{0:T(128)S(1)} all-reduce(f32[128]{0:T(128)S(1)} %multiply_reduce_fusion.2), channel_id=1, replica_groups=mesh['groups'=2,'dp'=16] {'dp'}, use_global_device_ids=true, to_apply=%region_20.21 | all-reduce | flops 128 | bytes 1024 | tf_op jit(solution)/shard_map/psum | solution.py:83
  528.5 29.7 %psum.70 = f32[128]{0:T(128)S(1)} all-reduce(f32[128]{0:T(128)S(1)} %multiply_reduce_fusion.1), channel_id=1, replica_groups=mesh['groups'=2,'dp'=16] {'dp'}, use_global_device_ids=true, to_apply=%region_22.23 | all-reduce | flops 128 | bytes 1024 | tf_op jit(solution)/shard_map/psum | solution.py:83
  559.2 17.4 %fusion.37 = f32[8192,128]{1,0:T(8,128)} fusion(f32[8192,512]{1,0:T(8,128)} %copy-done.1, f32[512,128]{1,0:T(8,128)S(1)} %multiply_add_fusion.1), kind=kOutput, calls=%fused_computation.74 | convolution fusion | flops 6442450944 | bytes 21233664 | tf_op jit(solution)/shard_map/dot_general | solution.py:122
  578.5 67.9 %reduce-scatter.11.cloned.1.call-done = f32[512,128]{1,0:T(8,128)} async-done(((f32[8192,128]{1,0:T(8,128)}), f32[512,128]{1,0:T(8,128)}) %reduce-scatter.11.cloned.1.call-update) | async-done | bytes 262160 | tf_op jit(solution)/shard_map/reduce_scatter | solution.py:121
  647.5 30.2 %psum.71 = f32[128]{0:T(128)S(1)} all-reduce(f32[128]{0:T(128)S(1)} %multiply_reduce_fusion), channel_id=1, replica_groups=mesh['groups'=2,'dp'=16] {'dp'}, use_global_device_ids=true, to_apply=%region_25.26 | all-reduce | flops 128 | bytes 1024 | tf_op jit(solution)/shard_map/psum | solution.py:83
  678.0 57.6 %all-reduce = f32[32,128]{1,0:T(8,128)S(1)} all-reduce(f32[32,128]{1,0:T(8,128)S(1)} %convolution_multiply_fusion), channel_id=6, replica_groups=mesh['groups'=2,'dp'=16] {'dp'}, use_global_device_ids=true, to_apply=%region_26.27.clone | all-reduce | flops 4096 | bytes 32768
  (101 shorter events, 49.5 us)
Async XLA Ops:
  7.2 190.7 %reduce-scatter.5.cloned.1.call-start = ((), (), s32[]{:S(2)}) async-start(), calls=%async_computation.4 | async-start | bytes 4456448 | tf_op jit(solution)/shard_map/reduce_scatter | solution.py:121
  17.1 33.7 %copy-start.13 = (s32[128]{0:T(128)S(1)}, s32[128]{0:T(128)}, u32[]{:S(2)}) copy-start(s32[128]{0:T(128)} %param.18) | copy-start | bytes 1540
  19.5 7.1 collective-permute-start
  20.0 6.7 collective-permute-start.8
  26.6 6.0 collective-permute-start.1
  26.7 6.0 collective-permute-start.9
  32.7 6.0 collective-permute-start.2
  32.7 6.0 collective-permute-start.10
  38.7 6.0 collective-permute-start.3
  38.8 6.0 collective-permute-start.11
  44.7 6.0 collective-permute-start.4
  44.8 6.0 collective-permute-start.12
  50.8 6.0 collective-permute-start.5
  50.8 6.0 collective-permute-start.13
  56.8 6.0 collective-permute-start.6
  56.9 41.4 %copy-start.7 = (bf16[2,8192]{1,0:T(2,128)(2,1)}, bf16[2,8192]{1,0:T(2,128)(2,1)S(1)}, u32[]{:S(2)}) copy-start(bf16[2,8192]{1,0:T(2,128)(2,1)S(1)} %collective-permute-done.13) | copy-start | bytes 98308
  56.9 41.4 %collective-permute-start.14 = (bf16[2,8192]{1,0:T(2,128)(2,1)S(1)}, bf16[2,8192]{1,0:T(2,128)(2,1)S(1)}, u32[]{:S(2)}, u32[]{:S(2)}) collective-permute-start(bf16[2,8192]{1,0:T(2,128)(2,1)S(1)} %collective-permute-done.13), channel_id=1, source_target_pairs={{0,15},{1,0},{2,1},{3,2},{4,3},{5,4},{6,5},{7,6},{8,7},{9,8},{10,9... | collective-permute-start | bytes 98312 | tf_op jit(solution)/shard_map/ppermute | solution.py:22
  62.8 35.4 %copy-start.8 = (bf16[2,8192]{1,0:T(2,128)(2,1)}, bf16[2,8192]{1,0:T(2,128)(2,1)S(1)}, u32[]{:S(2)}) copy-start(bf16[2,8192]{1,0:T(2,128)(2,1)S(1)} %collective-permute-done.6) | copy-start | bytes 98308
  62.8 36.0 %collective-permute-start.7 = (bf16[2,8192]{1,0:T(2,128)(2,1)S(1)}, bf16[2,8192]{1,0:T(2,128)(2,1)}, u32[]{:S(2)}, u32[]{:S(2)}) collective-permute-start(bf16[2,8192]{1,0:T(2,128)(2,1)S(1)} %collective-permute-done.6), channel_id=1, source_target_pairs={{0,1},{1,2},{2,3},{3,4},{4,5},{5,6},{6,7},{7,8},{8,9},{9,10},{10,1... | collective-permute-start | bytes 98312 | tf_op jit(solution)/shard_map/ppermute | solution.py:20
  127.6 219.3 %reduce-scatter.7.cloned.1.call-start = ((), (), s32[]{:S(2)}) async-start(), calls=%async_computation.5 | async-start | bytes 4456448 | tf_op jit(solution)/shard_map/reduce_scatter | solution.py:121
  277.2 69.7 %copy-start.2 = (f32[512,128]{1,0:T(8,128)S(1)}, f32[512,128]{1,0:T(8,128)}, u32[]{:S(2)}) copy-start(f32[512,128]{1,0:T(8,128)} %reduce-scatter.5.cloned.1.call-done) | copy-start | bytes 786436
  277.3 219.1 %reduce-scatter.9.cloned.1.call-start = ((), (), s32[]{:S(2)}) async-start(), calls=%async_computation.6 | async-start | bytes 4456448 | tf_op jit(solution)/shard_map/reduce_scatter | solution.py:121
  426.2 220.2 %reduce-scatter.11.cloned.1.call-start = ((), (), s32[]{:S(2)}) async-start(), calls=%async_computation.7 | async-start | bytes 4456448 | tf_op jit(solution)/shard_map/reduce_scatter | solution.py:121
  677.7 58.4 %copy-start.5 = (f32[512,128]{1,0:T(8,128)}, f32[512,128]{1,0:T(8,128)S(1)}, u32[]{:S(2)}) copy-start(f32[512,128]{1,0:T(8,128)S(1)} %fusion.21) | copy-start | bytes 786436
  (10 other events, 52.7 us)
Sparse Core Ops, SparseCore 0:
  127.8 70.1 reduce-scatter.4
  277.4 69.5 reduce-scatter.6
  426.4 69.9 reduce-scatter.8
  576.8 69.6 reduce-scatter.10
